TPU v7x, 32 devices: a whole 2x2x4 slice. The times are simulated.
32 devices in a mesh: fsdp: 4 (over y, core), ctx: 2 (over x), tp: 4 (over z).
Axes of the slice: x: 2, y: 2, z: 4, core: 2. Of those that a mesh axis runs over, the one named last changes fastest.
Arguments:
- inputs: bfloat16 [32, 320, 1024], P('fsdp', 'ctx'), may hold values from -6 to 6
- cotangent: bfloat16 [32, 320, 1024], P('fsdp', 'ctx'), may hold values from -6 to 6
- visible: int32 [32, 320], P('fsdp'), may hold values from 0 to 1, as said below
- w_qkv: float32 [1024, 3, 1024], P('fsdp', None, 'tp'), may hold values from -0.1875 to 0.1875
- b_qv: float32 [2, 1024], P(None, 'tp'), may hold values from -3 to 3
- w_out: float32 [1024, 1024], P('tp', 'fsdp'), may hold values from -0.75 to 0.75
- b_out: float32 [1024], replicated, may hold values from -3 to 3
- w_up: float32 [1024, 4096], P('fsdp', 'tp'), may hold values from -0.1875 to 0.1875
- b_up: float32 [4096], P('tp'), may hold values from -3 to 3
- w_down: float32 [4096, 1024], P('tp', 'fsdp'), may hold values from -0.09375 to 0.09375
- b_down: float32 [1024], replicated, may hold values from -3 to 3
- gain_one: float32 [1024], replicated, may hold values from 0.1 to 1.9
- shift_one: float32 [1024], replicated, may hold values from -3 to 3
- gain_two: float32 [1024], replicated, may hold values from 0.1 to 1.9
- shift_two: float32 [1024], replicated, may hold values from -3 to 3
Outputs:
- output: float32 [32, 320, 1024], P('fsdp', 'ctx')
- grad_inputs: float32 [32, 320, 1024], P('fsdp', 'ctx')
- grad_w_qkv: float32 [1024, 3, 1024], P('fsdp', None, 'tp')
- grad_b_qv: float32 [2, 1024], P(None, 'tp')
- grad_w_out: float32 [1024, 1024], P('tp', 'fsdp')
- grad_b_out: float32 [1024], replicated
- grad_w_up: float32 [1024, 4096], P('fsdp', 'tp')
- grad_b_up: float32 [4096], P('tp')
- grad_w_down: float32 [4096, 1024], P('tp', 'fsdp')
- grad_b_down: float32 [1024], replicated
- grad_gain_one: float32 [1024], replicated
- grad_shift_one: float32 [1024], replicated
- grad_gain_two: float32 [1024], replicated
- grad_shift_two: float32 [1024], replicated
Inputs may be any that keep to these rules, and one draw needn't show every extreme that they name: `visible`: the first 64 tokens of every image are 1; of the 256 image tokens of each image between a tenth and two fifths are 0.
All inputs are finite; a program needn't handle non-finite values.
Results may differ from a plain program's by a relative error of at most 0.012.
Values may be sent and summed in bfloat16 or wider, within the bound.
No kernel may reach another device: no remote copies, remote signals or barrier semaphores. Data moves between devices by JAX's collectives and lax.ppermute only.
A program may use at most 192 MiB of HBM per device.

v0:
```python
import jax
import jax.numpy as jnp
from jax import lax
from jax.sharding import PartitionSpec as P

HEAD = 64
EPSILON = 1e-06


def layer_norm(values, gain, shift):
    center = values - jnp.mean(values, axis=-1, keepdims=True)
    spread = jnp.mean(center * center, axis=-1, keepdims=True)
    return center * lax.rsqrt(spread + EPSILON) * gain + shift


def gelu_exact(values):
    return jax.nn.gelu(values, approximate=False)


def head_total(partial_sum):
    return lax.psum(partial_sum, "tp")


def attend(queries, keys_all, values_all, key_keep, scale_factor):
    scores = (
        jnp.einsum("iqhe,ikhe->ihqk", queries, keys_all, preferred_element_type=jnp.float32)
        * scale_factor
    )
    scores = jnp.where(key_keep, scores, -1e30)
    row_max = jnp.max(scores, axis=-1, keepdims=True)
    exponent = jnp.exp(scores - row_max)
    row_total = jnp.sum(exponent, axis=-1, keepdims=True)
    log_total = row_max + jnp.log(row_total)
    probability = exponent / row_total
    mixed = jnp.einsum(
        "ihqk,ikhe->iqhe",
        probability.astype(jnp.bfloat16),
        values_all,
        preferred_element_type=jnp.float32,
    )
    return (mixed, log_total)


def attend_back(queries, keys_all, values_all, key_keep, log_total, grad_mixed, scale_factor):
    again = (
        jnp.einsum("iqhe,ikhe->ihqk", queries, keys_all, preferred_element_type=jnp.float32)
        * scale_factor
    )
    again = jnp.where(key_keep, again, -1e30)
    prob_again = jnp.exp(again - log_total)
    grad_probs = jnp.einsum(
        "iqhe,ikhe->ihqk", grad_mixed, values_all, preferred_element_type=jnp.float32
    )
    grad_values = jnp.einsum(
        "ihqk,iqhe->ikhe",
        prob_again.astype(jnp.bfloat16),
        grad_mixed,
        preferred_element_type=jnp.float32,
    )
    grad_scores = prob_again * (
        grad_probs - jnp.sum(grad_probs * prob_again, axis=-1, keepdims=True)
    )
    grad_scores_low = grad_scores.astype(jnp.bfloat16)
    grad_queries = (
        jnp.einsum("ihqk,ikhe->iqhe", grad_scores_low, keys_all, preferred_element_type=jnp.float32)
        * scale_factor
    )
    grad_keys = (
        jnp.einsum("ihqk,iqhe->ikhe", grad_scores_low, queries, preferred_element_type=jnp.float32)
        * scale_factor
    )
    return (grad_queries, grad_keys, grad_values)


def on_device(
    inputs,
    cotangent,
    visible,
    w_qkv,
    b_qv,
    w_out,
    b_out,
    w_up,
    b_up,
    w_down,
    b_down,
    gain_one,
    shift_one,
    gain_two,
    shift_two,
):
    images, row_count, model_width = inputs.shape
    seq_total = visible.shape[1]
    tokens = images * row_count
    scale_factor = HEAD ** (-0.5)
    first_row = lax.axis_index("ctx") * row_count
    row_keep = (
        lax.dynamic_slice_in_dim(visible, first_row, row_count, 1)
        .astype(jnp.float32)
        .reshape(tokens, 1)
    )
    key_keep = (visible > 0)[:, None, None, :]
    qkv_w, out_w, up_w, down_w = (
        lax.all_gather(w_qkv.astype(jnp.bfloat16), "fsdp", axis=0, tiled=True),
        lax.all_gather(w_out.astype(jnp.bfloat16), "fsdp", axis=1, tiled=True),
        lax.all_gather(w_up.astype(jnp.bfloat16), "fsdp", axis=0, tiled=True),
        lax.all_gather(w_down.astype(jnp.bfloat16), "fsdp", axis=1, tiled=True),
    )
    local_width = qkv_w.shape[2]
    local_heads = local_width // HEAD
    flat_in = inputs.astype(jnp.float32).reshape(tokens, model_width)
    normed, norm_one_back = jax.vjp(layer_norm, flat_in, gain_one, shift_one)
    normed_low = normed.astype(jnp.bfloat16)
    bias_all = jnp.stack([b_qv[0], jnp.zeros_like(b_qv[0]), b_qv[1]])
    projected = (
        jnp.einsum("td,dcf->tcf", normed_low, qkv_w, preferred_element_type=jnp.float32) + bias_all
    )
    projected_low = projected.astype(jnp.bfloat16)
    queries = projected_low[:, 0].reshape(images, row_count, local_heads, HEAD)
    keys_here = projected_low[:, 1].reshape(images, row_count, local_width)
    values_here = projected_low[:, 2].reshape(images, row_count, local_width)
    keys_all, values_all = (
        lax.all_gather(keys_here, "ctx", axis=1, tiled=True),
        lax.all_gather(values_here, "ctx", axis=1, tiled=True),
    )
    keys_all = keys_all.reshape(images, seq_total, local_heads, HEAD)
    values_all = values_all.reshape(images, seq_total, local_heads, HEAD)
    mixed_heads, log_total = attend(queries, keys_all, values_all, key_keep, scale_factor)
    mixed_low = mixed_heads.astype(jnp.bfloat16).reshape(tokens, local_width)
    attended = head_total(jnp.dot(mixed_low, out_w, preferred_element_type=jnp.float32)) + b_out
    residual = flat_in + attended
    normed_two, norm_two_back = jax.vjp(layer_norm, residual, gain_two, shift_two)
    normed_two_low = normed_two.astype(jnp.bfloat16)
    hidden = jnp.dot(normed_two_low, up_w, preferred_element_type=jnp.float32) + b_up
    active, gelu_back = jax.vjp(gelu_exact, hidden)
    active_low = active.astype(jnp.bfloat16)
    branch = head_total(jnp.dot(active_low, down_w, preferred_element_type=jnp.float32)) + b_down
    result = row_keep * (residual + branch)
    grad_out = cotangent.astype(jnp.float32).reshape(tokens, model_width) * row_keep
    grad_branch = grad_out.astype(jnp.bfloat16)
    down_grad = jnp.dot(active_low.T, grad_branch, preferred_element_type=jnp.float32)
    down_bias_grad = jnp.sum(grad_branch.astype(jnp.float32), axis=0)
    grad_active = jnp.dot(grad_branch, down_w.T, preferred_element_type=jnp.float32)
    (grad_hidden,) = gelu_back(grad_active)
    grad_hidden_low = grad_hidden.astype(jnp.bfloat16)
    up_bias_grad = jnp.sum(grad_hidden_low.astype(jnp.float32), axis=0)
    up_grad = jnp.dot(normed_two_low.T, grad_hidden_low, preferred_element_type=jnp.float32)
    grad_normed_two = head_total(
        jnp.dot(grad_hidden_low, up_w.T, preferred_element_type=jnp.float32)
    )
    grad_resid_norm, gain_two_grad, shift_two_grad = norm_two_back(grad_normed_two)
    grad_resid = grad_out + grad_resid_norm
    grad_attended = grad_resid.astype(jnp.bfloat16)
    out_bias_grad = jnp.sum(grad_attended.astype(jnp.float32), axis=0)
    out_grad = jnp.dot(mixed_low.T, grad_attended, preferred_element_type=jnp.float32)
    grad_mixed_low = jnp.dot(grad_attended, out_w.T, preferred_element_type=jnp.float32).astype(
        jnp.bfloat16
    )
    grad_mixed = grad_mixed_low.reshape(images, row_count, local_heads, HEAD)
    grad_queries, grad_keys, grad_values = attend_back(
        queries, keys_all, values_all, key_keep, log_total, grad_mixed, scale_factor
    )
    grad_keys_here, grad_values_here = (
        lax.psum_scatter(
            grad_keys.reshape(images, seq_total, local_width),
            "ctx",
            scatter_dimension=1,
            tiled=True,
        ),
        lax.psum_scatter(
            grad_values.reshape(images, seq_total, local_width),
            "ctx",
            scatter_dimension=1,
            tiled=True,
        ),
    )
    grad_projected = jnp.stack(
        [
            grad_queries.reshape(tokens, local_width),
            grad_keys_here.reshape(tokens, local_width),
            grad_values_here.reshape(tokens, local_width),
        ],
        axis=1,
    ).astype(jnp.bfloat16)
    qv_bias_grad = jnp.sum(grad_projected.astype(jnp.float32)[:, 0::2], axis=0)
    qkv_grad = jnp.einsum(
        "td,tcf->dcf", normed_low, grad_projected, preferred_element_type=jnp.float32
    )
    grad_normed = head_total(
        jnp.einsum("tcf,dcf->td", grad_projected, qkv_w, preferred_element_type=jnp.float32)
    )
    grad_input_norm, gain_one_grad, shift_one_grad = norm_one_back(grad_normed)
    grad_input = (grad_resid + grad_input_norm).reshape(images, row_count, model_width)
    spread = (
        lax.psum_scatter(qkv_grad, "fsdp", scatter_dimension=0, tiled=True),
        lax.psum_scatter(out_grad, "fsdp", scatter_dimension=1, tiled=True),
        lax.psum_scatter(up_grad, "fsdp", scatter_dimension=0, tiled=True),
        lax.psum_scatter(down_grad, "fsdp", scatter_dimension=1, tiled=True),
    )
    qkv_total, out_total, up_total, down_total = lax.psum(
        (spread[0], spread[1], spread[2], spread[3]), "ctx"
    )
    small = lax.psum(
        (
            qv_bias_grad,
            out_bias_grad,
            up_bias_grad,
            down_bias_grad,
            gain_one_grad,
            shift_one_grad,
            gain_two_grad,
            shift_two_grad,
        ),
        ("fsdp", "ctx"),
    )
    return (
        result.reshape(images, row_count, model_width),
        grad_input,
        qkv_total,
        small[0],
        out_total,
        small[1],
        up_total,
        small[2],
        down_total,
        small[3],
        small[4],
        small[5],
        small[6],
        small[7],
    )


def solution(mesh):
    placed = (
        P("fsdp", "ctx", None),
        P("fsdp", "ctx", None),
        P("fsdp", None),
        P("fsdp", None, "tp"),
        P(None, "tp"),
        P("tp", "fsdp"),
        P(),
        P("fsdp", "tp"),
        P("tp"),
        P("tp", "fsdp"),
        P(),
        P(),
        P(),
        P(),
        P(),
    )
    return jax.shard_map(
        on_device,
        mesh=mesh,
        in_specs=placed,
        out_specs=(
            P("fsdp", "ctx", None),
            P("fsdp", "ctx", None),
            P("fsdp", None, "tp"),
            P(None, "tp"),
            P("tp", "fsdp"),
            P(),
            P("fsdp", "tp"),
            P("tp"),
            P("tp", "fsdp"),
            P(),
            P(),
            P(),
            P(),
            P(),
        ),
        check_vma=False,
    )
```

profile of v0, /device:TPU:0, one launch (start us, length us, event | category | flops | bytes accessed | tf_op | source)
XLA Modules:
  0.0 1293.8 jit_solution(9456932758075033936)
XLA Ops:
  15.6 17.0 %all-gather.6.cloned.1.call-done = bf16[1024,3,256]{2,0,1:T(8,128)(2,1)} async-done(((bf16[256,3,256]{2,0,1:T(8,128)(2,1)}), bf16[1024,3,256]{2,0,1:T(8,128)(2,1)}) %all-gather.6.cloned.1.call-update) | async-done | bytes 1572880 | tf_op jit(solution)/shard_map/all_gather | solution.py:104
  38.3 7.6 all_gather.21
  51.2 11.4 all-gather.10.cloned.1.call-done
  74.6 14.4 %all-gather.8.cloned.1.call-done = bf16[8,320,256]{2,1,0:T(8,128)(2,1)} async-done(((bf16[8,160,256]{2,1,0:T(8,128)(2,1)}), bf16[8,320,256]{2,1,0:T(8,128)(2,1)}) %all-gather.8.cloned.1.call-update) | async-done | bytes 1310736 | tf_op jit(solution)/shard_map/all_gather | solution.py:124
  91.6 5.1 fusion.30
  109.5 4.5 fusion.19
  114.0 179.8 %all-reduce.8.cloned.1.call-done = f32[1280,1024]{1,0:T(8,128)} async-done(((f32[1280,1024]{1,0:T(8,128)}), f32[1280,1024]{1,0:T(8,128)}) %all-reduce.8.cloned.1.call-update) | async-done | bytes 5242896 | tf_op jit(solution)/shard_map/psum | solution.py:21
  300.1 17.3 %all-gather.12.cloned.1.call-done = bf16[1024,1024]{1,0:T(8,128)(2,1)} async-done(((bf16[256,1024]{1,0:T(8,128)(2,1)}), bf16[1024,1024]{1,0:T(8,128)(2,1)}) %all-gather.12.cloned.1.call-update) | async-done | bytes 2097168 | tf_op jit(solution)/shard_map/all_gather | solution.py:106
  317.4 8.5 fusion.39
  325.9 16.3 %all-gather.14.cloned.1.call-done = bf16[1024,1024]{1,0:T(8,128)(2,1)} async-done(((bf16[1024,256]{1,0:T(8,128)(2,1)}), bf16[1024,1024]{1,0:T(8,128)(2,1)}) %all-gather.14.cloned.1.call-update) | async-done | bytes 2097168 | tf_op jit(solution)/shard_map/all_gather | solution.py:107
  342.3 18.4 %convert_reduce_fusion.2 = (f32[1024]{0:T(1024)S(1)}, bf16[1280,1024]{1,0:T(8,128)(2,1)S(1)}, f32[1280,1024]{1,0:T(8,128)}) fusion(f32[1280,1024]{1,0:T(8,128)} %fusion.39, f32[1024]{0:T(1024)S(1)} %copy-done.29, bf16[1280,1024]{1,0:T(8,128)(2,1)} %fusion.19, bf16[1024,1024]{1,0:T(8,128)(2,1)} %all-gather.14.cloned.1.call-done), kind=kOutput, calls=%fused_computation.31 | convolution fusion | flops 2782657536 | bytes 17833984 | tf_op jit(solution)/shard_map/dot_general | solution.py:143
  362.1 4.7 fusion.49
  367.3 188.6 %all-reduce.10.cloned.1.call-done = f32[1280,1024]{1,0:T(8,128)} async-done(((f32[1280,1024]{1,0:T(8,128)}), f32[1280,1024]{1,0:T(8,128)}) %all-reduce.10.cloned.1.call-update) | async-done | bytes 5242896 | tf_op jit(solution)/shard_map/psum | solution.py:21
  555.9 5.2 multiply_reduce_fusion.1
  577.5 7.2 fusion.20
  588.4 7.3 multiply_reduce_fusion
  595.8 5.4 multiply_convert_fusion
  611.4 5.6 multiply_convert_fusion.2
  618.5 4.5 fusion.51
  623.1 8.6 fusion.38
  632.0 6.2 fusion.31
  646.2 18.7 %reduce-scatter.7.cloned.1.call-done = f32[8,160,256]{2,0,1:T(8,128)} async-done(((f32[8,320,256]{2,0,1:T(8,128)}), f32[8,160,256]{2,0,1:T(8,128)}) %reduce-scatter.7.cloned.1.call-update) | async-done | bytes 1310736 | tf_op jit(solution)/shard_map/reduce_scatter | solution.py:164
  667.3 5.8 fusion.26
  673.2 8.0 fusion.48
  681.2 4.6 convolution_bitcast_fusion
  692.8 47.2 %reduce-scatter.17.cloned.1.call-done = f32[1024,256]{1,0:T(8,128)} async-done(((f32[1024,1024]{1,0:T(8,128)}), f32[1024,256]{1,0:T(8,128)}) %reduce-scatter.17.cloned.1.call-update) | async-done | bytes 1048592 | tf_op jit(solution)/shard_map/reduce_scatter | solution.py:198
  740.0 46.9 %reduce-scatter.15.cloned.1.call-done = f32[256,1024]{1,0:T(8,128)} async-done(((f32[1024,1024]{1,0:T(8,128)}), f32[256,1024]{1,0:T(8,128)}) %reduce-scatter.15.cloned.1.call-update) | async-done | bytes 1048592 | tf_op jit(solution)/shard_map/reduce_scatter | solution.py:197
  787.0 40.7 %reduce-scatter.11.cloned.1.call-done = f32[256,3,256]{2,0,1:T(8,128)} async-done(((f32[1024,3,256]{2,0,1:T(8,128)}), f32[256,3,256]{2,0,1:T(8,128)}) %reduce-scatter.11.cloned.1.call-update) | async-done | bytes 786448 | tf_op jit(solution)/shard_map/reduce_scatter | solution.py:195
  827.7 362.2 %all-reduce.12.cloned.1.call-done = (f32[1280,1024]{1,0:T(8,128)}, f32[1280,1024]{1,0:T(8,128)}) async-done(((f32[1280,1024]{1,0:T(8,128)}, f32[1280,1024]{1,0:T(8,128)}), (f32[1280,1024]{1,0:T(8,128)}, f32[1280,1024]{1,0:T(8,128)})) %all-reduce.12.cloned.1.call-update) | async-done | bytes 10485776 | tf_op jit(solution)/shard_map/psum | solution.py:21
  1196.9 25.6 %all-reduce = (f32[2,256]{1,0:T(2,128)}, f32[1024]{0:T(1024)}, f32[1024]{0:T(1024)}, f32[1024]{0:T(1024)}, f32[1024]{0:T(1024)}, /*index=5*/f32[1024]{0:T(1024)}, f32[1024]{0:T(1024)}, f32[1024]{0:T(1024)}) all-reduce(f32[2,256]{1,0:T(2,128)S(1)} %convert_reduce_fusion.4, ...), channel_id=1, replica_groups=mesh['fsdp'=4,'ctx'=2,'tp'=4] {'fsdp','ctx'}, use_global_device_ids=true, to_apply=%region_20.21 | all-reduce | flops 7680 | bytes 61440 | tf_op jit(solution)/shard_map/psum | solution.py:203
  1222.5 13.8 %add_add_fusion.2 = (f32[1280,1024]{1,0:T(8,128)}, f32[1280,1024]{1,0:T(8,128)}) fusion(f32[1280,1024]{1,0:T(8,128)} %copy-done.4, bf16[8,160,1024]{2,1,0:T(8,128)(2,1)} %param.16, f32[1280]{0:T(1024)S(1)} %negate_multiply_fusion.1, f32[1280]{0:T(1024)S(1)} %negate_multiply_fusion.2, f32[1280]{0:T(1024)S(1)} %mul.190, f32[1280]{0:T(1024)S(1)} %multiply_multiply_fusion.5, ...), kind=kLoop, calls=%fused_computation.33 | loop fusion | flops 20971520 | bytes 36739072 | tf_op jit(solution)/shard_map/add | solution.py:193
  1236.3 42.5 %all-reduce.14.cloned.1.call-done = (f32[256,3,256]{2,0,1:T(8,128)}, f32[256,256]{1,0:T(8,128)}, f32[256,1024]{1,0:T(8,128)}, f32[1024,256]{1,0:T(8,128)}) async-done(((f32[256,3,256]{2,0,1:T(8,128)}, f32[256,256]{1,0:T(8,128)}, f32[256,1024]{1,0:T(8,128)}, f32[1024,256]{1,0:T(8,128)}), (f32[256,3,256]{2,0,1:T(8,128)}, f32[256,256]{1,0:T(8,128)}, f32[256,1024]{1,0:T(8,128)}, ...) | async-done | bytes 3145744 | tf_op jit(solution)/shard_map/psum | solution.py:200
  (166 shorter events, 119.3 us)
Async XLA Ops:
  7.2 25.4 %all-gather.6.cloned.1.call-start = ((), (), s32[]{:S(2)}) async-start(), calls=%async_computation.6 | async-start | bytes 1966080 | tf_op jit(solution)/shard_map/all_gather | solution.py:104
  9.4 53.3 %all-gather.10.cloned.1.call-start = ((), (), s32[]{:S(2)}) async-start(), calls=%async_computation.8 | async-start | bytes 1966080 | tf_op jit(solution)/shard_map/all_gather | solution.py:123
  11.7 20.9 %copy-start.17 = (f32[1280]{0:T(1024)}, f32[1280]{0:T(1024)S(1)}, u32[]{:S(2)}) copy-start(f32[1280]{0:T(1024)S(1)} %div.47) | copy-start | bytes 15364
  12.6 20.0 %copy-start.21 = (f32[1280]{0:T(1024)}, f32[1280]{0:T(1024)S(1)}, u32[]{:S(2)}) copy-start(f32[1280]{0:T(1024)S(1)} %add.140) | copy-start | bytes 15364
  15.6 22.7 %copy-start.16 = (f32[256,256]{1,0:T(8,128)S(1)}, f32[256,256]{1,0:T(8,128)}, u32[]{:S(2)}) copy-start(f32[256,256]{1,0:T(8,128)} %param.20) | copy-start | bytes 786436
  37.0 9.2 copy-start.25
  38.2 50.8 %all-gather.8.cloned.1.call-start = ((), (), s32[]{:S(2)}) async-start(), calls=%async_computation.7 | async-start | bytes 1966080 | tf_op jit(solution)/shard_map/all_gather | solution.py:124
  46.0 247.8 %all-reduce.8.cloned.1.call-start = ((), (), s32[]{:S(2)}) async-start(), calls=%async_computation.9 | async-start | bytes 10485760 | tf_op jit(solution)/shard_map/psum | solution.py:21
  104.7 189.1 %copy-start.28 = (f32[1024]{0:T(1024)S(1)}, f32[1024]{0:T(1024)}, u32[]{:S(2)}) copy-start(f32[1024]{0:T(1024)} %param.21) | copy-start | bytes 12292
  104.8 212.6 %all-gather.12.cloned.1.call-start = ((), (), s32[]{:S(2)}) async-start(), calls=%async_computation.10 | async-start | bytes 2621440 | tf_op jit(solution)/shard_map/all_gather | solution.py:106
  106.9 235.3 %all-gather.14.cloned.1.call-start = ((), (), s32[]{:S(2)}) async-start(), calls=%async_computation.11 | async-start | bytes 2621440 | tf_op jit(solution)/shard_map/all_gather | solution.py:107
  109.1 446.8 %all-reduce.10.cloned.1.call-start = ((), (), s32[]{:S(2)}) async-start(), calls=%async_computation.12 | async-start | bytes 10485760 | tf_op jit(solution)/shard_map/psum | solution.py:21
  297.1 20.3 %copy-start.26 = (f32[1024]{0:T(1024)S(1)}, f32[1024]{0:T(1024)}, u32[]{:S(2)}) copy-start(f32[1024]{0:T(1024)} %param.28) | copy-start | bytes 12292
  297.1 20.3 %copy-start.34 = (f32[1024]{0:T(1024)S(1)}, f32[1024]{0:T(1024)}, u32[]{:S(2)}) copy-start(f32[1024]{0:T(1024)} %param.29) | copy-start | bytes 12292
  300.1 42.2 %copy-start.29 = (f32[1024]{0:T(1024)S(1)}, f32[1024]{0:T(1024)}, u32[]{:S(2)}) copy-start(f32[1024]{0:T(1024)} %param.23) | copy-start | bytes 12292
  342.3 19.8 %copy-start.32 = (bf16[1024,1024]{1,0:T(8,128)(2,1)S(1)}, bf16[1024,1024]{1,0:T(8,128)(2,1)}, u32[]{:S(2)}) copy-start(bf16[1024,1024]{1,0:T(8,128)(2,1)} %all-gather.12.cloned.1.call-done) | copy-start | bytes 6291460
  366.8 277.9 %reduce-scatter.9.cloned.1.call-start = ((), (), s32[]{:S(2)}) async-start(), calls=%async_computation.14 | async-start | bytes 3932160 | tf_op jit(solution)/shard_map/reduce_scatter | solution.py:170
  588.2 76.7 %reduce-scatter.7.cloned.1.call-start = ((), (), s32[]{:S(2)}) async-start(), calls=%async_computation.13 | async-start | bytes 3932160 | tf_op jit(solution)/shard_map/reduce_scatter | solution.py:164
  607.7 85.1 %reduce-scatter.13.cloned.1.call-start = ((), (), s32[]{:S(2)}) async-start(), calls=%async_computation.16 | async-start | bytes 1310720 | tf_op jit(solution)/shard_map/reduce_scatter | solution.py:196
  611.3 128.7 %reduce-scatter.17.cloned.1.call-start = ((), (), s32[]{:S(2)}) async-start(), calls=%async_computation.18 | async-start | bytes 5242880 | tf_op jit(solution)/shard_map/reduce_scatter | solution.py:198
  623.1 163.9 %reduce-scatter.15.cloned.1.call-start = ((), (), s32[]{:S(2)}) async-start(), calls=%async_computation.17 | async-start | bytes 5242880 | tf_op jit(solution)/shard_map/reduce_scatter | solution.py:197
  631.8 195.9 %reduce-scatter.11.cloned.1.call-start = ((), (), s32[]{:S(2)}) async-start(), calls=%async_computation.15 | async-start | bytes 3932160 | tf_op jit(solution)/shard_map/reduce_scatter | solution.py:195
  673.1 516.7 %all-reduce.12.cloned.1.call-start = ((), (), s32[]{:S(2)}) async-start(), calls=%async_computation.19 | async-start | bytes 20971520 | tf_op jit(solution)/shard_map/psum | solution.py:21
  673.2 8.0 copy-start.13
  673.2 8.0 copy-start.14
  673.2 8.0 copy-start.33
  685.8 504.1 %copy-start.18 = (f32[1280]{0:T(1024)S(1)}, f32[1280]{0:T(1024)}, u32[]{:S(2)}) copy-start(f32[1280]{0:T(1024)} %copy-done.17) | copy-start | bytes 15364
  685.8 504.1 %copy-start.24 = (f32[1024]{0:T(1024)S(1)}, f32[1024]{0:T(1024)}, u32[]{:S(2)}) copy-start(f32[1024]{0:T(1024)} %param.26) | copy-start | bytes 12292
  685.8 592.9 %all-reduce.14.cloned.1.call-start = ((), (), s32[]{:S(2)}) async-start(), calls=%async_computation.20 | async-start | bytes 6291456 | tf_op jit(solution)/shard_map/psum | solution.py:200
  827.6 366.1 %copy-start.22 = (f32[1280]{0:T(1024)S(1)}, f32[1280]{0:T(1024)}, u32[]{:S(2)}) copy-start(f32[1280]{0:T(1024)} %copy-done.21) | copy-start | bytes 15364
  827.6 366.1 %copy-start.20 = (f32[1280]{0:T(1024)S(1)}, f32[1280]{0:T(1024)}, u32[]{:S(2)}) copy-start(f32[1280]{0:T(1024)} %copy-done.19) | copy-start | bytes 15364
  1193.7 28.8 %copy-start.30 = (f32[1024]{0:T(1024)S(1)}, f32[1024]{0:T(1024)}, u32[]{:S(2)}) copy-start(f32[1024]{0:T(1024)} %param.25) | copy-start | bytes 12292
  (19 other events, 69.1 us)
Sparse Core Ops, SparseCore 0:
  10.2 22.3 all-gather.5
  38.3 24.2 all-gather.9
  64.7 24.2 all-gather.7
  104.9 188.8 all-reduce.7
  295.8 21.5 all-gather.11
  319.4 22.8 all-gather.13
  366.9 188.9 all-reduce.9
  588.3 36.5 reduce-scatter.8
  627.3 37.5 reduce-scatter.6
  667.8 24.8 reduce-scatter.12
  695.5 44.5 reduce-scatter.16
  742.4 44.5 reduce-scatter.14
  789.7 37.9 reduce-scatter.10
  830.7 359.1 all-reduce.11
  1192.2 86.5 all-reduce.13
where the time goes:
time: 1300 us; the launch traced here: 1290 us
  waiting for transfers between devices  1010 us (78%)
  matrix products  110 us (8%)
  other arithmetic  71.5 us (6%)
  local copies, waits for them, and re-layouts  56.8 us (4%)
  blocking collectives  33.2 us (3%)
  between operations  14.7 us (1%)
    psum x3, waiting for transfers between devices, head_total(): return lax.psum(partial_sum, 'tp')  731 us
    reduce_scatter x1, waiting for transfers between devices, on_device(): lax.psum_scatter(down_grad, 'fsdp', scatter_dimension=1, tiled=True)  47.2 us
    reduce_scatter x1, waiting for transfers between devices, on_device(): lax.psum_scatter(up_grad, 'fsdp', scatter_dimension=0, tiled=True)  46.9 us
    psum x1, waiting for transfers between devices, on_device(): lax.psum((spread[0], spread[1], spread[2], spread[3]), 'ctx')  42.5 us
    reduce_scatter x1, waiting for transfers between devices, on_device(): lax.psum_scatter(qkv_grad, 'fsdp', scatter_dimension=0, tiled=True)  40.7 us
  transfers between devices with their start and end apart: 15, of which 14 were waited for; matrix products, arithmetic and copies ran while one was open for 11% of the time, Pallas kernels for 0%

commit v1 on v0

--- a/solution.py
+++ b/solution.py
@@ -18,7 +18,7 @@
 
 
 def head_total(partial_sum):
-    return lax.psum(partial_sum, "tp")
+    return jnp.sum(lax.all_gather(partial_sum, "tp"), axis=0)
 
 
 def attend(queries, keys_all, values_all, key_keep, scale_factor):

time: 1300 us -> 2010 us (1.55)
  waiting for transfers between devices: 1010 us -> 1640 us
  other arithmetic: 71.5 us -> 142 us
    all_gather x0 -> x4, waiting for transfers between devices: none -> 1360 us  [head_total(): return jnp.sum(lax.all_gather(partial_sum, 'tp'), axis=0)]
    psum x3 -> x0, waiting for transfers between devices: 731 us -> none  [head_total(): return lax.psum(partial_sum, 'tp')]
    reduce_sum x1 -> x4, other arithmetic: 2.32 us -> 46.4 us  [head_total(): return jnp.sum(lax.all_gather(partial_sum, 'tp'), axis=0)]
    reduce_scatter x1, waiting for transfers between devices: 47.2 us -> 18 us  [on_device(): lax.psum_scatter(down_grad, 'fsdp', scatter_dimension=1, tiled=True)]
    reduce_scatter x1, waiting for transfers between devices: 2.59 us -> 28 us  [on_device(): lax.psum_scatter(out_grad, 'fsdp', scatter_dimension=1, tiled=True)]
  transfers between devices with their start and end apart: 15 -> 16, of which waited for: 14 -> 15; matrix products, arithmetic and copies ran while one was open for 11% -> 10% of each run, Pallas kernels for 0% -> 0%
where the time goes in v1:
time: 2010 us; the launch traced here: 2000 us
  waiting for transfers between devices  1640 us (82%)
  other arithmetic  142 us (7%)
  matrix products  110 us (5%)
  local copies, waits for them, and re-layouts  54 us (3%)
  blocking collectives  33 us (2%)
    all_gather x4, waiting for transfers between devices, head_total(): return jnp.sum(lax.all_gather(partial_sum, 'tp'), axis=0)  1360 us
    reduce_scatter x1, waiting for transfers between devices, on_device(): lax.psum_scatter(up_grad, 'fsdp', scatter_dimension=0, tiled=True)  47.2 us
    psum x1, waiting for transfers between devices, on_device(): lax.psum((spread[0], spread[1], spread[2], spread[3]), 'ctx')  46.5 us
    reduce_sum x4, other arithmetic, head_total(): return jnp.sum(lax.all_gather(partial_sum, 'tp'), axis=0)  46.4 us
    reduce_scatter x1, waiting for transfers between devices, on_device(): lax.psum_scatter(qkv_grad, 'fsdp', scatter_dimension=0, tiled=True)  40.4 us
  transfers between devices with their start and end apart: 16, of which 15 were waited for; matrix products, arithmetic and copies ran while one was open for 10% of the time, Pallas kernels for 0%

profile of v1, /device:TPU:0, one launch (start us, length us, event | category | flops | bytes accessed | tf_op | source)
XLA Modules:
  0.0 2000.8 jit_solution(4406925769418027453)
XLA Ops:
  16.7 15.9 all-gather.14.cloned.1.call-done
  39.5 7.6 all_gather.45
  52.5 11.3 all-gather.18.cloned.1.call-done
  75.6 14.6 all-gather.16.cloned.1.call-done
  115.2 348.0 %all-gather.24.cloned.1.call-done = f32[5120,1024]{1,0:T(8,128)} async-done(((f32[1280,1024]{1,0:T(8,128)}), f32[5120,1024]{1,0:T(8,128)}) %all-gather.24.cloned.1.call-update) | async-done | bytes 20971536 | tf_op jit(solution)/shard_map/all_gather | solution.py:21
  463.2 11.3 reduce_sum.243
  487.9 7.6 fusion.40
  495.5 15.7 all-gather.22.cloned.1.call-done
  511.2 18.4 convert_reduce_fusion.1
  548.0 344.7 %all-gather.28.cloned.1.call-done = f32[5120,1024]{1,0:T(8,128)} async-done(((f32[1280,1024]{1,0:T(8,128)}), f32[5120,1024]{1,0:T(8,128)}) %all-gather.28.cloned.1.call-update) | async-done | bytes 20971536 | tf_op jit(solution)/shard_map/all_gather | solution.py:21
  892.8 12.5 reduce_sum.249
  911.3 338.5 %all-gather.26.cloned.1.call-done = f32[5120,1024]{1,0:T(8,128)} async-done(((f32[1280,1024]{1,0:T(8,128)}), f32[5120,1024]{1,0:T(8,128)}) %all-gather.26.cloned.1.call-update) | async-done | bytes 20971536 | tf_op jit(solution)/shard_map/all_gather | solution.py:21
  1249.8 11.0 reduce_sum.247
  1260.8 9.4 fusion.35
  1282.3 7.2 fusion.13
  1293.3 7.3 multiply_reduce_fusion
  1330.9 38.3 %reduce-scatter.7.cloned.1.call-done = f32[8,160,256]{2,0,1:T(8,128)} async-done(((f32[8,320,256]{2,0,1:T(8,128)}), f32[8,160,256]{2,0,1:T(8,128)}) %reduce-scatter.7.cloned.1.call-update) | async-done | bytes 1310736 | tf_op jit(solution)/shard_map/reduce_scatter | solution.py:164
  1371.5 6.2 convolution_bitcast_fusion
  1378.2 7.7 fusion.45
  1386.0 8.7 fusion.44
  1394.8 7.5 fusion.30
  1402.6 332.2 %all-gather.30.cloned.1.call-done = f32[5120,1024]{1,0:T(8,128)} async-done(((f32[1280,1024]{1,0:T(8,128)}), f32[5120,1024]{1,0:T(8,128)}) %all-gather.30.cloned.1.call-update) | async-done | bytes 20971536 | tf_op jit(solution)/shard_map/all_gather | solution.py:21
  1734.8 11.5 reduce_sum.255
  1753.2 7.2 convert_reduce_fusion.2
  1762.3 18.0 reduce-scatter.17.cloned.1.call-done
  1780.3 47.2 %reduce-scatter.15.cloned.1.call-done = f32[256,1024]{1,0:T(8,128)} async-done(((f32[1024,1024]{1,0:T(8,128)}), f32[256,1024]{1,0:T(8,128)}) %reduce-scatter.15.cloned.1.call-update) | async-done | bytes 1048592 | tf_op jit(solution)/shard_map/reduce_scatter | solution.py:197
  1827.5 40.4 %reduce-scatter.11.cloned.1.call-done = f32[256,3,256]{2,0,1:T(8,128)} async-done(((f32[1024,3,256]{2,0,1:T(8,128)}), f32[256,3,256]{2,0,1:T(8,128)}) %reduce-scatter.11.cloned.1.call-update) | async-done | bytes 786448 | tf_op jit(solution)/shard_map/reduce_scatter | solution.py:195
  1867.9 28.0 %reduce-scatter.13.cloned.1.call-done = f32[256,256]{1,0:T(8,128)} async-done(((f32[256,1024]{1,0:T(8,128)}), f32[256,256]{1,0:T(8,128)}) %reduce-scatter.13.cloned.1.call-update) | async-done | bytes 262160 | tf_op jit(solution)/shard_map/reduce_scatter | solution.py:196
  1895.9 8.2 reduce_sum.266
  1905.8 8.2 reduce_sum.264
  1913.9 25.3 %all-reduce = (f32[2,256]{1,0:T(2,128)}, f32[1024]{0:T(1024)}, f32[1024]{0:T(1024)}, f32[1024]{0:T(1024)}, f32[1024]{0:T(1024)}, /*index=5*/f32[1024]{0:T(1024)}, f32[1024]{0:T(1024)}, f32[1024]{0:T(1024)}) all-reduce(f32[2,256]{1,0:T(2,128)S(1)} %convert_reduce_fusion.4, ...), channel_id=1, replica_groups=mesh['fsdp'=4,'ctx'=2,'tp'=4] {'fsdp','ctx'}, use_global_device_ids=true, to_apply=%region_20.21 | all-reduce | flops 7680 | bytes 61440 | tf_op jit(solution)/shard_map/psum | solution.py:203
  1939.3 46.5 %all-reduce.4.cloned.1.call-done = (f32[256,3,256]{2,0,1:T(8,128)}, f32[256,256]{1,0:T(8,128)}, f32[256,1024]{1,0:T(8,128)}, f32[1024,256]{1,0:T(8,128)}) async-done(((f32[256,3,256]{2,0,1:T(8,128)}, f32[256,256]{1,0:T(8,128)}, f32[256,1024]{1,0:T(8,128)}, f32[1024,256]{1,0:T(8,128)}), (f32[256,3,256]{2,0,1:T(8,128)}, f32[256,256]{1,0:T(8,128)}, f32[256,1024]{1,0:T(8,128)}, ...) | async-done | bytes 3145744 | tf_op jit(solution)/shard_map/psum | solution.py:200
  (182 shorter events, 163.9 us)
Async XLA Ops:
  7.2 25.4 %all-gather.14.cloned.1.call-start = ((), (), s32[]{:S(2)}) async-start(), calls=%async_computation.6 | async-start | bytes 1966080 | tf_op jit(solution)/shard_map/all_gather | solution.py:104
  9.3 54.5 %all-gather.18.cloned.1.call-start = ((), (), s32[]{:S(2)}) async-start(), calls=%async_computation.8 | async-start | bytes 1966080 | tf_op jit(solution)/shard_map/all_gather | solution.py:123
  11.6 20.9 %copy-start.24 = (f32[1280]{0:T(1024)}, f32[1280]{0:T(1024)S(1)}, u32[]{:S(2)}) copy-start(f32[1280]{0:T(1024)S(1)} %div.57) | copy-start | bytes 15364
  11.7 20.9 %copy-start.20 = (f32[1024]{0:T(1024)S(1)}, f32[1024]{0:T(1024)}, u32[]{:S(2)}) copy-start(f32[1024]{0:T(1024)} %param.26) | copy-start | bytes 12292
  11.7 20.9 %copy-start.34 = (f32[1024]{0:T(1024)S(1)}, f32[1024]{0:T(1024)}, u32[]{:S(2)}) copy-start(f32[1024]{0:T(1024)} %param.27) | copy-start | bytes 12292
  13.1 19.4 copy-start.15
  13.2 19.3 copy-start.26
  16.7 22.8 %copy-start.14 = (f32[256,256]{1,0:T(8,128)S(1)}, f32[256,256]{1,0:T(8,128)}, u32[]{:S(2)}) copy-start(f32[256,256]{1,0:T(8,128)} %param.20) | copy-start | bytes 786436
  38.2 9.3 copy-start.23
  39.4 50.8 %all-gather.16.cloned.1.call-start = ((), (), s32[]{:S(2)}) async-start(), calls=%async_computation.7 | async-start | bytes 1966080 | tf_op jit(solution)/shard_map/all_gather | solution.py:124
  47.1 416.1 %all-gather.24.cloned.1.call-start = ((), (), s32[]{:S(2)}) async-start(), calls=%async_computation.17 | async-start | bytes 26214400 | tf_op jit(solution)/shard_map/all_gather | solution.py:21
  106.2 381.7 %all-gather.20.cloned.1.call-start = ((), (), s32[]{:S(2)}) async-start(), calls=%async_computation.9 | async-start | bytes 2621440 | tf_op jit(solution)/shard_map/all_gather | solution.py:106
  108.4 402.9 %all-gather.22.cloned.1.call-start = ((), (), s32[]{:S(2)}) async-start(), calls=%async_computation.10 | async-start | bytes 2621440 | tf_op jit(solution)/shard_map/all_gather | solution.py:107
  110.5 782.2 %all-gather.28.cloned.1.call-start = ((), (), s32[]{:S(2)}) async-start(), calls=%async_computation.19 | async-start | bytes 26214400 | tf_op jit(solution)/shard_map/all_gather | solution.py:21
  463.2 11.3 copy-start.22
  487.9 23.3 %copy-start.29 = (f32[1024]{0:T(1024)S(1)}, f32[1024]{0:T(1024)}, u32[]{:S(2)}) copy-start(f32[1024]{0:T(1024)} %param.23) | copy-start | bytes 12292
  511.2 19.8 copy-start.33
  535.8 714.0 %all-gather.26.cloned.1.call-start = ((), (), s32[]{:S(2)}) async-start(), calls=%async_computation.18 | async-start | bytes 26214400 | tf_op jit(solution)/shard_map/all_gather | solution.py:21
  548.0 781.4 %reduce-scatter.9.cloned.1.call-start = ((), (), s32[]{:S(2)}) async-start(), calls=%async_computation.12 | async-start | bytes 3932160 | tf_op jit(solution)/shard_map/reduce_scatter | solution.py:170
  1249.8 11.0 copy-start.30
  1293.0 76.1 %reduce-scatter.7.cloned.1.call-start = ((), (), s32[]{:S(2)}) async-start(), calls=%async_computation.11 | async-start | bytes 3932160 | tf_op jit(solution)/shard_map/reduce_scatter | solution.py:164
  1312.6 422.1 %all-gather.30.cloned.1.call-start = ((), (), s32[]{:S(2)}) async-start(), calls=%async_computation.20 | async-start | bytes 26214400 | tf_op jit(solution)/shard_map/all_gather | solution.py:21
  1377.8 402.5 %reduce-scatter.17.cloned.1.call-start = ((), (), s32[]{:S(2)}) async-start(), calls=%async_computation.16 | async-start | bytes 5242880 | tf_op jit(solution)/shard_map/reduce_scatter | solution.py:198
  1385.9 8.9 copy-start.21
  1385.9 8.9 copy-start.25
  1385.9 8.9 copy-start.27
  1386.0 8.9 copy-start.35
  1386.0 441.5 %reduce-scatter.15.cloned.1.call-start = ((), (), s32[]{:S(2)}) async-start(), calls=%async_computation.15 | async-start | bytes 5242880 | tf_op jit(solution)/shard_map/reduce_scatter | solution.py:197
  1394.7 473.2 %reduce-scatter.11.cloned.1.call-start = ((), (), s32[]{:S(2)}) async-start(), calls=%async_computation.13 | async-start | bytes 3932160 | tf_op jit(solution)/shard_map/reduce_scatter | solution.py:195
  1402.4 493.5 %reduce-scatter.13.cloned.1.call-start = ((), (), s32[]{:S(2)}) async-start(), calls=%async_computation.14 | async-start | bytes 1310720 | tf_op jit(solution)/shard_map/reduce_scatter | solution.py:196
  1734.8 11.5 copy-start.13
  1762.3 223.5 %all-reduce.4.cloned.1.call-start = ((), (), s32[]{:S(2)}) async-start(), calls=%async_computation.21 | async-start | bytes 6291456 | tf_op jit(solution)/shard_map/psum | solution.py:200
  (21 other events, 85.9 us)
Sparse Core Ops, SparseCore 0:
  10.2 22.3 all-gather.13
  39.5 24.2 all-gather.17
  65.9 24.2 all-gather.15
  106.3 356.8 all-gather.23
  465.2 21.1 all-gather.19
  488.4 22.8 all-gather.21
  535.9 356.8 all-gather.27
  894.4 355.4 all-gather.25
  1293.2 36.1 reduce-scatter.8
  1331.5 37.5 reduce-scatter.6
  1377.9 356.8 all-gather.29
  1737.1 43.0 reduce-scatter.16
  1783.0 44.4 reduce-scatter.14
  1829.9 37.9 reduce-scatter.10
  1871.0 24.8 reduce-scatter.12
  1898.2 87.5 all-reduce.3
